TPU v7x, 512 devices: a whole 4x4x16 slice. The times are simulated.
512 devices in a mesh: row: 16 (over x, y), col: 32 (over z, core).
Axes of the slice: x: 4, y: 4, z: 16, core: 2. Of those that a mesh axis runs over, the one named last changes fastest.
Arguments:
- front: bfloat16 [16384, 16384], P('row', 'col'), may hold values from -0.046875 to 0.046875
- diag_inverse: float32 [128, 128, 128], P('row'), may hold values from -0.25 to 1.5
- load: float32 [8, 16384], P(None, 'row'), may hold values from -6 to 6
- panel_order: int32 [128], replicated, may hold values from 0 to 127, each once
- tie: float32 [32, 16384], P('col', 'row'), may hold values from 0.5 to 1.5
- mass: float32 [32, 16384], P('col', 'row'), may hold values from 0.5 to 6
- modes: bfloat16 [1024, 32, 16384], P(None, 'col', 'row'), may hold values from -0.0234375 to 0.0234375
Outputs:
- front_solution: float32 [8, 16384], P(None, 'row')
- residual_vectors: float32 [8, 32, 16384], P(None, 'col', 'row')
All inputs are finite; a program needn't handle non-finite values.
Results may differ from a plain program's by a relative error of at most 0.0049.
Values may be sent and summed in bfloat16 or wider, within the bound.
No kernel may reach another device: no remote copies, remote signals or barrier semaphores. Data moves between devices by JAX's collectives and lax.ppermute only.
A program may use at most 64 MiB of HBM per device.

v0:
```python
import jax
import jax.numpy as jnp
from jax import lax
from jax.sharding import PartitionSpec as P

LEVELS = 4
highest = lax.Precision.HIGHEST


def on_device(front, diag_inverse, load, panel_order, tie, mass, modes):
    vectors = load.shape[0]
    block_size = diag_inverse.shape[1]
    local_panels = diag_inverse.shape[0]
    rows_local = front.shape[0]
    cols_local = front.shape[1]
    panels = panel_order.shape[0]
    row_at = lax.axis_index("row")
    col_at = lax.axis_index("col")
    counting = jnp.arange(panels, dtype=jnp.int32)
    matches = panel_order[:, None] == counting[None, :]
    ranks = jnp.sum(jnp.where(matches, counting[:, None], 0), axis=0)
    levels_of = ranks // (panels // LEVELS)
    position_level = jnp.repeat(levels_of, block_size)
    row_level = lax.dynamic_slice_in_dim(position_level, row_at * rows_local, rows_local, 0)
    pending = jnp.zeros((vectors, rows_local), jnp.float32)
    forward_out = jnp.zeros((vectors, rows_local), jnp.float32)
    for level in range(LEVELS):
        if level > 0:
            total_sum = lax.psum(pending, "col")
        else:
            total_sum = pending
        remain = (load - total_sum).reshape(vectors, local_panels, block_size)
        candidate = jnp.einsum("vpj,pij->vpi", remain, diag_inverse, precision=highest).reshape(
            vectors, rows_local
        )
        chosen = row_level[None, :] == level
        forward_out = jnp.where(chosen, candidate, forward_out)
        if level < LEVELS - 1:
            fresh = jnp.where(chosen, forward_out, 0.0).astype(jnp.bfloat16)
            whole = lax.all_gather(fresh, "row", axis=1, tiled=True)
            mine = lax.dynamic_slice_in_dim(whole, col_at * cols_local, cols_local, 1)
            pending = pending + jnp.dot(mine, front.T, preferred_element_type=jnp.float32)
    back_pending = jnp.zeros((vectors, cols_local), jnp.float32)
    back_out = jnp.zeros((vectors, rows_local), jnp.float32)
    for level in reversed(range(LEVELS)):
        if level < LEVELS - 1:
            column_sum = lax.psum(back_pending, "row")
            full_sum = lax.all_gather(column_sum, "col", axis=1, tiled=True)
            here = lax.dynamic_slice_in_dim(full_sum, row_at * rows_local, rows_local, 1)
        else:
            here = jnp.zeros((vectors, rows_local), jnp.float32)
        remain = (forward_out - here).reshape(vectors, local_panels, block_size)
        candidate = jnp.einsum("vpj,pji->vpi", remain, diag_inverse, precision=highest).reshape(
            vectors, rows_local
        )
        chosen = row_level[None, :] == level
        back_out = jnp.where(chosen, candidate, back_out)
        if level > 0:
            fresh = jnp.where(chosen, back_out, 0.0).astype(jnp.bfloat16)
            back_pending = back_pending + jnp.dot(fresh, front, preferred_element_type=jnp.float32)
    static = tie[None, :, :] * back_out[:, None, :]
    weighted = (mass[None, :, :] * static).astype(jnp.bfloat16).reshape(vectors, -1)
    mode_rows = modes.reshape(modes.shape[0], -1)
    partial_coords = lax.dot_general(
        weighted, mode_rows, (((1,), (1,)), ((), ())), preferred_element_type=jnp.float32
    )
    coords = lax.psum(partial_coords, ("row", "col"))
    correction = jnp.dot(coords.astype(jnp.bfloat16), mode_rows, preferred_element_type=jnp.float32)
    return (back_out, static - correction.reshape(static.shape))


def solution(mesh):
    in_specs = (
        P("row", "col"),
        P("row", None, None),
        P(None, "row"),
        P(),
        P("col", "row"),
        P("col", "row"),
        P(None, "col", "row"),
    )
    out_specs = (P(None, "row"), P(None, "col", "row"))
    return jax.shard_map(
        on_device, mesh=mesh, in_specs=in_specs, out_specs=out_specs, check_vma=False
    )
```

profile of v0, /device:TPU:1, one launch (start us, length us, event | category | flops | bytes accessed | tf_op | source)
XLA Modules:
  0.0 765.4 jit_solution(5559178636949547583)
XLA Ops:
  0.7 0.9 select_reduce_fusion
  1.7 2.0 select_convert_fusion.5
  3.7 19.7 %all_gather.18 = bf16[8,16384]{1,0:T(8,128)(2,1)S(1)} all-gather(bf16[8,1024]{1,0:T(8,128)(2,1)S(1)} %get-tuple-element.14), channel_id=1, replica_groups=mesh['row'=16,'col'=32] {'row'}, dimensions={1}, use_global_device_ids=true | all-gather | bytes 278528 | tf_op jit(solution)/shard_map/all_gather | solution.py:40
  23.3 1.6 fusion.64
  24.9 99.0 %psum.49 = f32[8,1024]{1,0:T(8,128)S(1)} all-reduce(f32[8,1024]{1,0:T(8,128)S(1)} %fusion.64), channel_id=1, replica_groups=mesh['row'=16,'col'=32] {'col'}, use_global_device_ids=true, to_apply=%region_1.2 | all-reduce | flops 8192 | bytes 65536 | tf_op jit(solution)/shard_map/psum | solution.py:29
  123.9 2.0 select_convert_fusion.4
  125.9 17.9 %all_gather.19 = bf16[8,16384]{1,0:T(8,128)(2,1)S(1)} all-gather(bf16[8,1024]{1,0:T(8,128)(2,1)S(1)} %get-tuple-element.8), channel_id=1, replica_groups=mesh['row'=16,'col'=32] {'row'}, dimensions={1}, use_global_device_ids=true | all-gather | bytes 278528 | tf_op jit(solution)/shard_map/all_gather | solution.py:40
  144.2 95.2 %psum.50 = f32[8,1024]{1,0:T(8,128)S(1)} all-reduce(f32[8,1024]{1,0:T(8,128)S(1)} %convolution_add_fusion.1), channel_id=1, replica_groups=mesh['row'=16,'col'=32] {'col'}, use_global_device_ids=true, to_apply=%region_2.3 | all-reduce | flops 8192 | bytes 65536 | tf_op jit(solution)/shard_map/psum | solution.py:29
  239.4 2.0 select_convert_fusion.3
  241.4 16.6 %all_gather.20 = bf16[8,16384]{1,0:T(8,128)(2,1)S(1)} all-gather(bf16[8,1024]{1,0:T(8,128)(2,1)S(1)} %get-tuple-element.17), channel_id=1, replica_groups=mesh['row'=16,'col'=32] {'row'}, dimensions={1}, use_global_device_ids=true | all-gather | bytes 278528 | tf_op jit(solution)/shard_map/all_gather | solution.py:40
  258.4 94.9 %psum.51 = f32[8,1024]{1,0:T(8,128)S(1)} all-reduce(f32[8,1024]{1,0:T(8,128)S(1)} %convolution_add_fusion), channel_id=1, replica_groups=mesh['row'=16,'col'=32] {'col'}, use_global_device_ids=true, to_apply=%region_3.4 | all-reduce | flops 8192 | bytes 65536 | tf_op jit(solution)/shard_map/psum | solution.py:29
  353.3 2.0 bitcast_select_fusion.5
  355.3 1.6 fusion.22
  357.1 58.2 %psum.52 = f32[8,512]{1,0:T(8,128)S(1)} all-reduce(f32[8,512]{1,0:T(8,128)S(1)} %fusion.40), channel_id=1, replica_groups=mesh['row'=16,'col'=32] {'row'}, use_global_device_ids=true, to_apply=%region_4.5 | all-reduce | flops 4096 | bytes 32768 | tf_op jit(solution)/shard_map/psum | solution.py:47
  415.3 45.4 %all_gather.21 = f32[8,16384]{1,0:T(8,128)S(1)} all-gather(f32[8,512]{1,0:T(8,128)S(1)} %psum.52), channel_id=1, replica_groups=mesh['row'=16,'col'=32] {'col'}, dimensions={1}, use_global_device_ids=true | all-gather | bytes 540672 | tf_op jit(solution)/shard_map/all_gather | solution.py:48
  460.8 1.6 bitcast_select_fusion.3
  462.6 55.9 %psum.53 = f32[8,512]{1,0:T(8,128)S(1)} all-reduce(f32[8,512]{1,0:T(8,128)S(1)} %convolution_add_fusion.3), channel_id=1, replica_groups=mesh['row'=16,'col'=32] {'row'}, use_global_device_ids=true, to_apply=%region_5.6 | all-reduce | flops 4096 | bytes 32768 | tf_op jit(solution)/shard_map/psum | solution.py:47
  518.5 44.6 %all_gather.22 = f32[8,16384]{1,0:T(8,128)S(1)} all-gather(f32[8,512]{1,0:T(8,128)S(1)} %psum.53), channel_id=1, replica_groups=mesh['row'=16,'col'=32] {'col'}, dimensions={1}, use_global_device_ids=true | all-gather | bytes 540672 | tf_op jit(solution)/shard_map/all_gather | solution.py:48
  563.1 1.6 fusion.18
  564.9 55.8 %psum.54 = f32[8,512]{1,0:T(8,128)S(1)} all-reduce(f32[8,512]{1,0:T(8,128)S(1)} %convolution_add_fusion.2), channel_id=1, replica_groups=mesh['row'=16,'col'=32] {'row'}, use_global_device_ids=true, to_apply=%region_6.7 | all-reduce | flops 4096 | bytes 32768 | tf_op jit(solution)/shard_map/psum | solution.py:47
  620.6 42.0 %all_gather.23 = f32[8,16384]{1,0:T(8,128)S(1)} all-gather(f32[8,512]{1,0:T(8,128)S(1)} %psum.54), channel_id=1, replica_groups=mesh['row'=16,'col'=32] {'col'}, dimensions={1}, use_global_device_ids=true | all-gather | bytes 540672 | tf_op jit(solution)/shard_map/all_gather | solution.py:48
  662.6 1.6 bitcast_select_fusion.1
  664.8 99.5 %psum.55 = bf16[8,1024]{1,0:T(8,128)(2,1)S(1)} all-reduce(f32[8,1024]{1,0:T(8,128)S(1)} %fusion.2), channel_id=1, replica_groups=mesh['row'=16,'col'=32] {'row','col'}, use_global_device_ids=true, to_apply=%region_7.8 | all-reduce | flops 8192 | bytes 49152 | tf_op jit(solution)/shard_map/psum | solution.py:67
  764.8 0.7 copy.11
  (22 shorter events, 2.6 us)
Async XLA Ops:
  0.6 663.6 %copy-start = (bf16[1024,1,1024]{2,0,1:T(8,128)(2,1)S(1)}, bf16[1024,1,1024]{2,0,1:T(8,128)(2,1)}, u32[]{:S(2)}) copy-start(bf16[1024,1,1024]{2,0,1:T(8,128)(2,1)} %param.13) | copy-start | bytes 6291460
  0.6 143.2 %copy-start.1 = (bf16[1024,512]{1,0:T(8,128)(2,1)S(1)}, bf16[1024,512]{1,0:T(8,128)(2,1)}, u32[]{:S(2)}) copy-start(bf16[1024,512]{1,0:T(8,128)(2,1)} %param.7) | copy-start | bytes 3145732
  0.7 123.3 %copy-start.2 = (f32[8,1024]{1,0:T(8,128)S(1)}, f32[8,1024]{1,0:T(8,128)}, u32[]{:S(2)}) copy-start(f32[8,1024]{1,0:T(8,128)} %param.9) | copy-start | bytes 98308
  462.6 201.6 %copy-start.4 = (f32[1,1024]{1,0:T(1,128)S(1)}, f32[1,1024]{1,0:T(1,128)}, u32[]{:S(2)}) copy-start(f32[1,1024]{1,0:T(1,128)} %param.11) | copy-start | bytes 12292
  462.6 201.6 %copy-start.5 = (f32[1,1024]{1,0:T(1,128)S(1)}, f32[1,1024]{1,0:T(1,128)}, u32[]{:S(2)}) copy-start(f32[1,1024]{1,0:T(1,128)} %param.12) | copy-start | bytes 12292
  664.2 100.6 %copy-start.3 = (f32[8,1024]{1,0:T(8,128)}, f32[8,1024]{1,0:T(8,128)S(1)}, u32[]{:S(2)}) copy-start(f32[8,1024]{1,0:T(8,128)S(1)} %get-tuple-element.23) | copy-start | bytes 98308
where the time goes:
time: 766 us; the launch traced here: 765 us
  blocking collectives  745 us (97%)
  matrix products  18.2 us (2%)
    psum x3, blocking collectives, on_device(): total_sum = lax.psum(pending, 'col')  289 us
    psum x3, blocking collectives, on_device(): column_sum = lax.psum(back_pending, 'row')  170 us
    all_gather x3, blocking collectives, on_device(): full_sum = lax.all_gather(column_sum, 'col', axis=1, tiled=True)  132 us
    psum x1, blocking collectives, on_device(): coords = lax.psum(partial_coords, ('row', 'col'))  99.5 us
    all_gather x3, blocking collectives, on_device(): whole = lax.all_gather(fresh, 'row', axis=1, tiled=True)  54.2 us

commit v1 on v0

--- a/solution.py
+++ b/solution.py
@@ -5,6 +5,21 @@
 
 LEVELS = 4
 highest = lax.Precision.HIGHEST
+
+
+def _touch_field(body, shard_axis):
+    n_parts = lax.psum(1, shard_axis)
+
+    def plane_proceed(w2, moved):
+        if moved >= n_parts:
+            return w2
+        even = range(n_parts)
+        carry_out = map(lambda it: (it, it ^ moved), even)
+        known = list(carry_out)
+        high = lax.ppermute(w2, shard_axis, known)
+        return plane_proceed(w2 + high, 2 * moved)
+
+    return plane_proceed(body, 1)
 
 
 def on_device(front, diag_inverse, load, panel_order, tie, mass, modes):
@@ -44,7 +59,7 @@
     back_out = jnp.zeros((vectors, rows_local), jnp.float32)
     for level in reversed(range(LEVELS)):
         if level < LEVELS - 1:
-            column_sum = lax.psum(back_pending, "row")
+            column_sum = _touch_field(back_pending, "row")
             full_sum = lax.all_gather(column_sum, "col", axis=1, tiled=True)
             here = lax.dynamic_slice_in_dim(full_sum, row_at * rows_local, rows_local, 1)
         else:

time: 766 us -> 629 us (0.82)
  blocking collectives: 745 us -> 548 us
  starting transfers between devices: 0 us -> 42.6 us
  waiting for transfers between devices: 0 us -> 20.5 us
    psum x3 -> x0, blocking collectives: 170 us -> none  [on_device(): column_sum = lax.psum(back_pending, 'row')]
    ppermute x0 -> x12, starting transfers between devices: none -> 42.6 us  [plane_proceed(): high = lax.ppermute(w2, shard_axis, known)]
    all_gather x3, blocking collectives: 132 us -> 104 us  [on_device(): full_sum = lax.all_gather(column_sum, 'col', axis=1, tiled=True)]
    ppermute x0 -> x12, waiting for transfers between devices: none -> 20.5 us  [plane_proceed(): high = lax.ppermute(w2, shard_axis, known)]
  transfers between devices with their start and end apart: 0 -> 12, of which waited for: 0 -> 12; matrix products, arithmetic and copies ran while one was open for 0% -> 0% of each run, Pallas kernels for 0% -> 0%
where the time goes in v1:
time: 629 us
  blocking collectives  548 us (87%)
  starting transfers between devices  42.6 us (7%)
  waiting for transfers between devices  20.5 us (3%)
  matrix products  15.2 us (2%)
    psum x3, blocking collectives, on_device(): total_sum = lax.psum(pending, 'col')  289 us
    all_gather x3, blocking collectives, on_device(): full_sum = lax.all_gather(column_sum, 'col', axis=1, tiled=True)  104 us
    psum x1, blocking collectives, on_device(): coords = lax.psum(partial_coords, ('row', 'col'))  100 us
    all_gather x3, blocking collectives, on_device(): whole = lax.all_gather(fresh, 'row', axis=1, tiled=True)  54.2 us
    ppermute x12, starting transfers between devices, plane_proceed(): high = lax.ppermute(w2, shard_axis, known)  42.6 us
    ppermute x12, waiting for transfers between devices, plane_proceed(): high = lax.ppermute(w2, shard_axis, known)  20.5 us
  transfers between devices with their start and end apart: 12, of which 12 were waited for; matrix products, arithmetic and copies ran while one was open for 0% of the time, Pallas kernels for 0%

profile of v1, /device:TPU:1, one launch (start us, length us, event | category | flops | bytes accessed | tf_op | source)
XLA Modules:
  0.0 628.5 jit_solution(14016891329895526743)
XLA Ops:
  3.7 19.7 %all_gather.18 = bf16[8,16384]{1,0:T(8,128)(2,1)S(1)} all-gather(bf16[8,1024]{1,0:T(8,128)(2,1)S(1)} %get-tuple-element.14), channel_id=1, replica_groups=mesh['row'=16,'col'=32] {'row'}, dimensions={1}, use_global_device_ids=true | all-gather | bytes 278528 | tf_op jit(solution)/shard_map/all_gather | solution.py:55
  24.9 99.0 %psum.28 = f32[8,1024]{1,0:T(8,128)S(1)} all-reduce(f32[8,1024]{1,0:T(8,128)S(1)} %fusion.64), channel_id=1, replica_groups=mesh['row'=16,'col'=32] {'col'}, use_global_device_ids=true, to_apply=%region_1.2 | all-reduce | flops 8192 | bytes 65536 | tf_op jit(solution)/shard_map/psum | solution.py:44
  125.9 17.9 %all_gather.19 = bf16[8,16384]{1,0:T(8,128)(2,1)S(1)} all-gather(bf16[8,1024]{1,0:T(8,128)(2,1)S(1)} %get-tuple-element.8), channel_id=1, replica_groups=mesh['row'=16,'col'=32] {'row'}, dimensions={1}, use_global_device_ids=true | all-gather | bytes 278528 | tf_op jit(solution)/shard_map/all_gather | solution.py:55
  144.2 95.2 %psum.29 = f32[8,1024]{1,0:T(8,128)S(1)} all-reduce(f32[8,1024]{1,0:T(8,128)S(1)} %convolution_add_fusion.1), channel_id=1, replica_groups=mesh['row'=16,'col'=32] {'col'}, use_global_device_ids=true, to_apply=%region_2.3 | all-reduce | flops 8192 | bytes 65536 | tf_op jit(solution)/shard_map/psum | solution.py:44
  241.4 16.6 %all_gather.20 = bf16[8,16384]{1,0:T(8,128)(2,1)S(1)} all-gather(bf16[8,1024]{1,0:T(8,128)(2,1)S(1)} %get-tuple-element.17), channel_id=1, replica_groups=mesh['row'=16,'col'=32] {'row'}, dimensions={1}, use_global_device_ids=true | all-gather | bytes 278528 | tf_op jit(solution)/shard_map/all_gather | solution.py:55
  258.4 94.9 %psum.30 = f32[8,1024]{1,0:T(8,128)S(1)} all-reduce(f32[8,1024]{1,0:T(8,128)S(1)} %convolution_add_fusion), channel_id=1, replica_groups=mesh['row'=16,'col'=32] {'col'}, use_global_device_ids=true, to_apply=%region_3.4 | all-reduce | flops 8192 | bytes 65536 | tf_op jit(solution)/shard_map/psum | solution.py:44
  353.3 2.0 bitcast_select_fusion.5
  357.2 2.8 collective-permute-start
  361.7 4.2 collective-permute-start.1
  367.7 2.8 collective-permute-start.2
  370.5 2.0 collective-permute-done.2
  372.5 4.2 collective-permute-start.3
  378.5 35.8 %all_gather.21 = f32[8,16384]{1,0:T(8,128)S(1)} all-gather(f32[8,512]{1,0:T(8,128)S(1)} %add.75), channel_id=1, replica_groups=mesh['row'=16,'col'=32] {'col'}, dimensions={1}, use_global_device_ids=true | all-gather | bytes 540672 | tf_op jit(solution)/shard_map/all_gather | solution.py:63
  415.1 3.0 collective-permute-start.4
  419.7 4.2 collective-permute-start.5
  425.7 2.9 collective-permute-start.6
  430.2 4.3 collective-permute-start.7
  436.1 35.4 %all_gather.22 = f32[8,16384]{1,0:T(8,128)S(1)} all-gather(f32[8,512]{1,0:T(8,128)S(1)} %add.80), channel_id=1, replica_groups=mesh['row'=16,'col'=32] {'col'}, dimensions={1}, use_global_device_ids=true | all-gather | bytes 540672 | tf_op jit(solution)/shard_map/all_gather | solution.py:63
  472.3 2.8 collective-permute-start.8
  476.8 4.2 collective-permute-start.9
  482.8 2.9 collective-permute-start.10
  487.3 4.3 collective-permute-start.11
  493.3 32.8 %all_gather.23 = f32[8,16384]{1,0:T(8,128)S(1)} all-gather(f32[8,512]{1,0:T(8,128)S(1)} %add.85), channel_id=1, replica_groups=mesh['row'=16,'col'=32] {'col'}, dimensions={1}, use_global_device_ids=true | all-gather | bytes 540672 | tf_op jit(solution)/shard_map/all_gather | solution.py:63
  527.3 100.2 %psum.31 = bf16[8,1024]{1,0:T(8,128)(2,1)S(1)} all-reduce(f32[8,1024]{1,0:T(8,128)S(1)} %fusion.2), channel_id=1, replica_groups=mesh['row'=16,'col'=32] {'row','col'}, use_global_device_ids=true, to_apply=%region_4.5 | all-reduce | flops 8192 | bytes 49152 | tf_op jit(solution)/shard_map/psum | solution.py:82
  (57 shorter events, 33.4 us)
Async XLA Ops:
  0.6 526.0 %copy-start = (bf16[1024,1,1024]{2,0,1:T(8,128)(2,1)S(1)}, bf16[1024,1,1024]{2,0,1:T(8,128)(2,1)}, u32[]{:S(2)}) copy-start(bf16[1024,1,1024]{2,0,1:T(8,128)(2,1)} %param.13) | copy-start | bytes 6291460
  0.6 123.3 %copy-start.3 = (f32[8,1024]{1,0:T(8,128)S(1)}, f32[8,1024]{1,0:T(8,128)}, u32[]{:S(2)}) copy-start(f32[8,1024]{1,0:T(8,128)} %param.9) | copy-start | bytes 98308
  0.7 143.2 %copy-start.1 = (bf16[1024,512]{1,0:T(8,128)(2,1)S(1)}, bf16[1024,512]{1,0:T(8,128)(2,1)}, u32[]{:S(2)}) copy-start(bf16[1024,512]{1,0:T(8,128)(2,1)} %param.7) | copy-start | bytes 3145732
  353.3 61.0 %copy-start.2 = (f32[8,128,128]{2,1,0:T(8,128)S(1)}, f32[8,128,128]{2,1,0:T(8,128)}, u32[]{:S(2)}) copy-start(f32[8,128,128]{2,1,0:T(8,128)} %param.8) | copy-start | bytes 1572868
  357.2 4.5 collective-permute-start
  361.7 6.0 collective-permute-start.1
  367.7 4.8 collective-permute-start.2
  372.5 6.0 collective-permute-start.3
  415.1 111.5 %copy-start.5 = (f32[1,1024]{1,0:T(1,128)S(1)}, f32[1,1024]{1,0:T(1,128)}, u32[]{:S(2)}) copy-start(f32[1,1024]{1,0:T(1,128)} %param.11) | copy-start | bytes 12292
  415.1 111.5 %copy-start.6 = (f32[1,1024]{1,0:T(1,128)S(1)}, f32[1,1024]{1,0:T(1,128)}, u32[]{:S(2)}) copy-start(f32[1,1024]{1,0:T(1,128)} %param.12) | copy-start | bytes 12292
  415.1 4.6 collective-permute-start.4
  419.7 6.0 collective-permute-start.5
  425.7 4.5 collective-permute-start.6
  430.2 6.0 collective-permute-start.7
  472.3 4.5 collective-permute-start.8
  476.8 6.0 collective-permute-start.9
  482.8 4.5 collective-permute-start.10
  487.3 6.0 collective-permute-start.11
  526.6 101.3 %copy-start.4 = (f32[8,1024]{1,0:T(8,128)}, f32[8,1024]{1,0:T(8,128)S(1)}, u32[]{:S(2)}) copy-start(f32[8,1024]{1,0:T(8,128)S(1)} %get-tuple-element.23) | copy-start | bytes 98308
